TPU v7x, 32 devices: a whole 2x2x4 slice. The times are simulated.
32 devices in a mesh: fsdp: 2 (over y), tensor: 4 (over x, core), replica: 4 (over z).
Axes of the slice: x: 2, y: 2, z: 4, core: 2. Of those that a mesh axis runs over, the one named last changes fastest.
Arguments:
- gradient: bfloat16 [4, 4096, 8192], P('replica', 'fsdp', 'tensor'), may hold values from -400 to 400, as said below
- momentum: float32 [4, 4096, 8192], P('replica', 'fsdp', 'tensor'), may hold values from -6 to 6
- basis: float32 [8192, 256], P('tensor', 'fsdp'), may hold values from -0.0625 to 0.0625
Outputs:
- update: bfloat16 [4096, 8192], P('fsdp', 'tensor')
- momentum_new: float32 [4, 4096, 8192], P('replica', 'fsdp', 'tensor')
- basis_new: float32 [8192, 256], P('tensor', 'fsdp')
Inputs may be any that keep to these rules, and one draw needn't show every extreme that they name: gradient entries are finite real numbers.
All inputs are finite; a program needn't handle non-finite values.
Results may differ from a plain program's by a relative error of at most 0.001.
Values sent between devices are 32-bit elements; how exact they have to be, the bound alone decides.
A program may use at most 128 MiB of HBM per device.

v0:
```python
import jax
import jax.numpy as jnp
from jax import lax
from jax.sharding import PartitionSpec as P

M_ROWS = 4096
NCOLS = 8192
RANK = 256
HIGH = lax.Precision.HIGHEST


def local(gradient, momentum, basis):
    replicas = lax.axis_size("replica")
    rank_local = basis.shape[1]
    buffer = momentum[0] + gradient[0].astype(jnp.float32)
    partial_value = jnp.dot(
        buffer,
        lax.all_gather(basis, "fsdp", axis=1, tiled=True),
        precision=HIGH,
        preferred_element_type=jnp.float32,
    )
    left = lax.psum(partial_value, ("tensor", "replica")) / replicas
    local_gram = jnp.dot(left.T, left, precision=HIGH, preferred_element_type=jnp.float32)
    gram = lax.psum(local_gram, "fsdp")
    chol = jnp.linalg.cholesky(gram)
    ortho = lax.linalg.triangular_solve(chol, left, left_side=False, lower=True, transpose_a=True)
    right_part = jnp.dot(buffer.T, ortho, precision=HIGH, preferred_element_type=jnp.float32)
    right = lax.psum(right_part, ("fsdp", "replica")) / replicas
    squares = lax.psum(jnp.sum(right * right, axis=0), "tensor")
    norms = jnp.sqrt(squares + 1e-12)
    basis_full = right / norms
    lowrank = jnp.dot(ortho, right.T, precision=HIGH, preferred_element_type=jnp.float32)
    momentum_new = (buffer - 0.05 * lowrank)[None]
    scale = (M_ROWS * NCOLS / RANK) ** 0.5
    update = (
        scale * jnp.dot(ortho, basis_full.T, precision=HIGH, preferred_element_type=jnp.float32)
    ).astype(jnp.bfloat16)
    offset = lax.axis_index("fsdp") * rank_local
    basis_new = lax.dynamic_slice_in_dim(basis_full, offset, rank_local, 1)
    return (update, momentum_new, basis_new)


def solution(mesh):
    return jax.shard_map(
        local,
        mesh=mesh,
        in_specs=(
            P("replica", "fsdp", "tensor"),
            P("replica", "fsdp", "tensor"),
            P("tensor", "fsdp"),
        ),
        out_specs=(P("fsdp", "tensor"), P("replica", "fsdp", "tensor"), P("tensor", "fsdp")),
        check_vma=False,
    )
```

profile of v0, /device:TPU:0, one launch (start us, length us, event | category | flops | bytes accessed | tf_op | source)
XLA Modules:
  0.0 472.0 jit_solution(12130268575645546304)
XLA Ops:
  7.2 0.0 all-gather.2.cloned.1.call-start
  7.2 0.7 all-gather.2.cloned.1.call-update
  7.9 0.0 all-reduce.5.cloned.1.call-start
  7.9 37.4 %all-gather.2.cloned.1.call-done = f32[2048,256]{1,0:T(8,128)} async-done(((f32[2048,128]{1,0:T(8,128)}), f32[2048,256]{1,0:T(8,128)}) %all-gather.2.cloned.1.call-update) | async-done | bytes 2097168 | tf_op jit(solution)/shard_map/all_gather | solution.py:18
  45.3 18.8 %fusion.2 = f32[2048,256]{1,0:T(8,128)} fusion(f32[2048,256]{1,0:T(8,128)} %all-gather.2.cloned.1.call-done, f32[1,2048,2048]{2,1,0:T(8,128)} %param.4, bf16[1,2048,2048]{2,1,0:T(8,128)(2,1)} %param.3), kind=kOutput, calls=%fused_computation.5 | convolution fusion | flops 12893290496 | bytes 29360128 | tf_op jit(solution)/shard_map/dot_general | solution.py:16
  64.2 0.0 all-reduce.5.cloned.1.call-update
  64.2 0.0 all-reduce.7.cloned.1.call-start
  64.3 98.4 %all-reduce.5.cloned.1.call-done = f32[2048,256]{1,0:T(8,128)} async-done(((f32[2048,256]{1,0:T(8,128)}), f32[2048,256]{1,0:T(8,128)}) %all-reduce.5.cloned.1.call-update) | async-done | bytes 2097168 | tf_op jit(solution)/shard_map/psum | solution.py:22
  162.6 6.4 %fusion.19 = f32[256,256]{0,1:T(8,128)} fusion(f32[2048,256]{1,0:T(8,128)} %all-reduce.5.cloned.1.call-done), kind=kOutput, calls=%fused_computation.47 | convolution fusion | flops 1611137024 | bytes 2359296 | tf_op jit(solution)/shard_map/dot_general | solution.py:23
  169.0 0.0 all-reduce.7.cloned.1.call-update
  169.1 0.6 all-reduce.9.cloned.1.call-start
  169.6 1.7 broadcast_multiply_fusion
  171.4 20.4 %all-reduce.7.cloned.1.call-done = f32[256,256]{0,1:T(8,128)} async-done(((f32[256,256]{0,1:T(8,128)}), f32[256,256]{0,1:T(8,128)}) %all-reduce.7.cloned.1.call-update) | async-done | bytes 262160 | tf_op jit(solution)/shard_map/psum | solution.py:24
  191.7 1.1 copy.7
  192.8 1.0 fusion.9
  193.8 11.7 %cholesky.50 = f32[128,128]{1,0:T(8,128)S(1)} custom-call(f32[128,128]{1,0:T(8,128)S(1)} %cholesky.118), custom_call_target="Cholesky" | custom-call | tf_op jit(solution)/shard_map/jit(cholesky)/cholesky | solution.py:25
  205.6 9.8 %custom-call.14 = f32[1,128,128]{1,2,0:T(8,128)S(1)} custom-call(f32[1,128,128]{2,1,0:T(8,128)S(1)} %get-tuple-element.24), custom_call_target="InvertDiagBlocksLowerTriangular" | custom-call | tf_op jit(solution)/shard_map/jit(cholesky)/cholesky | solution.py:25
  215.4 0.2 constant_dynamic-update-slice_fusion
  215.6 0.3 convolution_subtract_fusion.1
  215.9 11.7 %cholesky.105 = f32[128,128]{1,0:T(8,128)S(1)} custom-call(f32[128,128]{1,0:T(8,128)S(1)} %convolution_subtract_fusion.1), custom_call_target="Cholesky" | custom-call | tf_op jit(solution)/shard_map/jit(cholesky)/cholesky | solution.py:25
  227.6 0.6 compare_reduce_fusion
  229.6 0.1 triangular_solve.58
  229.7 4.2 while.1
  229.9 0.6 fusion.28
  230.5 1.4 bitcast_dynamic-update-slice_fusion.2
  231.9 0.6 fusion.28
  232.5 1.4 bitcast_dynamic-update-slice_fusion.2
  233.9 19.7 %custom-call.15 = f32[2,128,128]{1,2,0:T(8,128)S(1)} custom-call(f32[2,128,128]{2,1,0:T(8,128)S(1)} %get-tuple-element.10), custom_call_target="InvertDiagBlocksLowerTriangular" | custom-call | tf_op jit(solution)/shard_map/triangular_solve | solution.py:26
  253.5 1.1 fusion.6
  254.6 1.8 convolution_subtract_fusion
  256.5 1.1 fusion.10
  257.6 0.0 copy-start.1
  257.6 1.0 copy-done.1
  258.5 31.3 %fusion = f32[2048,256]{1,0:T(8,128)} fusion(f32[1,2048,2048]{2,1,0:T(8,128)} %param.4, bf16[1,2048,2048]{2,1,0:T(8,128)(2,1)} %param.3, f32[2048,128]{0,1:T(8,128)S(1)} %fusion.10, f32[2048,128]{0,1:T(8,128)S(1)} %fusion.6), kind=kOutput, calls=%fused_computation.3 | convolution fusion | flops 12893814784 | bytes 29360128 | tf_op jit(solution)/shard_map/dot_general | solution.py:27
  289.8 0.0 all-reduce.9.cloned.1.call-update
  289.8 102.4 %all-reduce.9.cloned.1.call-done = f32[2048,256]{1,0:T(8,128)} async-done(((f32[2048,256]{1,0:T(8,128)}), f32[2048,256]{1,0:T(8,128)}) %all-reduce.9.cloned.1.call-update) | async-done | bytes 2097168 | tf_op jit(solution)/shard_map/psum | solution.py:28
  392.3 0.0 copy-start
  392.3 2.0 multiply_reduce_fusion
  394.3 6.4 %psum.31 = f32[256]{0:T(256)S(1)} all-reduce(f32[256]{0:T(256)S(1)} %multiply_reduce_fusion), channel_id=1, replica_groups=mesh['fsdp'=2,'tensor'=4,'replica'=4] {'tensor'}, use_global_device_ids=true, to_apply=%region_8.9 | all-reduce | flops 256 | bytes 2048 | tf_op jit(solution)/shard_map/psum | solution.py:29
  400.7 0.0 copy-done
  400.7 0.0 copy-start.2
  400.7 0.1 multiply_divide_fusion
  400.9 1.1 copy-done.2
  401.9 28.8 %multiply_convert_fusion = bf16[2048,2048]{1,0:T(8,128)(2,1)} fusion(f32[2048,256]{1,0:T(8,128)S(1)} %multiply_divide_fusion, f32[2048,128]{0,1:T(8,128)S(1)} %copy-done.2, f32[2048,128]{0,1:T(8,128)S(1)} %fusion.6), kind=kOutput, calls=%fused_computation.8 | convolution fusion | flops 12893814784 | bytes 12582912 | tf_op jit(solution)/shard_map/dot_general | solution.py:36
  430.8 1.0 constant_dynamic-slice_fusion.1
  431.8 33.1 %fusion.4 = f32[1,2048,2048]{2,1,0:T(8,128)} fusion(f32[1,2048,2048]{2,1,0:T(8,128)} %param.4, bf16[1,2048,2048]{2,1,0:T(8,128)(2,1)} %param.3, f32[2048,256]{1,0:T(8,128)S(1)} %copy-done, f32[2048,128]{0,1:T(8,128)S(1)} %copy-done.2, f32[2048,128]{0,1:T(8,128)S(1)} %fusion.6), kind=kOutput, calls=%fused_computation.7 | convolution fusion | flops 12902727680 | bytes 46137344 | tf_op jit(solution)/shard_map/dot_general | solution.py:32
  (10 shorter events, 0.2 us)
Async XLA Ops:
  7.2 38.2 %all-gather.2.cloned.1.call-start = ((), (), s32[]{:S(2)}) async-start(), calls=%async_computation | async-start | bytes 3145728 | tf_op jit(solution)/shard_map/all_gather | solution.py:18
  7.9 154.7 %all-reduce.5.cloned.1.call-start = ((), (), s32[]{:S(2)}) async-start(), calls=%async_computation.1 | async-start | bytes 4194304 | tf_op jit(solution)/shard_map/psum | solution.py:22
  64.2 127.5 %all-reduce.7.cloned.1.call-start = ((), (), s32[]{:S(2)}) async-start(), calls=%async_computation.2 | async-start | bytes 524288 | tf_op jit(solution)/shard_map/psum | solution.py:24
  169.1 223.2 %all-reduce.9.cloned.1.call-start = ((), (), s32[]{:S(2)}) async-start(), calls=%async_computation.3 | async-start | bytes 4194304 | tf_op jit(solution)/shard_map/psum | solution.py:28
  257.6 1.0 copy-start.1
  392.3 8.4 %copy-start = (f32[2048,256]{1,0:T(8,128)S(1)}, f32[2048,256]{1,0:T(8,128)}, u32[]{:S(2)}) copy-start(f32[2048,256]{1,0:T(8,128)} %all-reduce.9.cloned.1.call-done) | copy-start | bytes 6291460
  400.7 1.2 copy-start.2
Sparse Core Ops, SparseCore 0:
  9.5 35.7 all-gather.1
  64.3 98.2 all-reduce.4
  169.2 22.4 all-reduce.6
  289.9 102.2 all-reduce.8
where the time goes:
time: 478 us; the launch traced here: 472 us
  waiting for transfers between devices  259 us (54%)
  matrix products  123 us (26%)
  other arithmetic  58.6 us (12%)
  between operations  15.7 us (3%)
  local copies, waits for them, and re-layouts  8.2 us (2%)
  blocking collectives  6.38 us (1%)
    psum x1, waiting for transfers between devices, local(): right = lax.psum(right_part, ('fsdp', 'replica')) / replicas  102 us
    psum x1, waiting for transfers between devices, local(): left = lax.psum(partial_value, ('tensor', 'replica')) / replicas  98.4 us
    all_gather x1, waiting for transfers between devices, local(): lax.all_gather(basis, 'fsdp', axis=1, tiled=True)  37.4 us
    another operation x6, other arithmetic, local(): chol = jnp.linalg.cholesky(gram)  34 us
    dot_general x1, matrix products, local(): jnp.dot(ortho, right.T, precision=HIGH, preferred_element_type=jnp.float32)  33.1 us
    dot_general x1, matrix products, local(): jnp.dot(buffer.T, ortho, precision=HIGH, preferred_element_type=jnp.float32)  31.3 us
    dot_general x1, matrix products, local(): jnp.dot(ortho, basis_full.T, precision=HIGH, preferred_element_type=jnp.f...  28.8 us
    psum x1, waiting for transfers between devices, local(): gram = lax.psum(local_gram, 'fsdp')  20.4 us
  transfers between devices with their start and end apart: 4, of which 4 were waited for; matrix products, arithmetic and copies ran while one was open for 0% of the time, Pallas kernels for 0%

commit v1 on v0

--- a/solution.py
+++ b/solution.py
@@ -25,7 +25,8 @@
     chol = jnp.linalg.cholesky(gram)
     ortho = lax.linalg.triangular_solve(chol, left, left_side=False, lower=True, transpose_a=True)
     right_part = jnp.dot(buffer.T, ortho, precision=HIGH, preferred_element_type=jnp.float32)
-    right = lax.psum(right_part, ("fsdp", "replica")) / replicas
+    lines_shape = lambda v0, shard_axis, mesh_dim: lax.psum(lax.psum(v0, shard_axis), mesh_dim)
+    right = lines_shape(right_part, "fsdp", "replica") / replicas
     squares = lax.psum(jnp.sum(right * right, axis=0), "tensor")
     norms = jnp.sqrt(squares + 1e-12)
     basis_full = right / norms

time: 478 us -> 528 us (1.10)
  waiting for transfers between devices: 259 us -> 308 us
    psum x1 -> x2, waiting for transfers between devices: 102 us -> 151 us  [the longest x1 88.4 us: local(): lax.psum(lax.psum(v0, shard_axis), mesh_dim)]
  transfers between devices with their start and end apart: 4 -> 5, of which waited for: 4 -> 5; matrix products, arithmetic and copies ran while one was open for 0% -> 0% of each run, Pallas kernels for 0% -> 0%
where the time goes in v1:
time: 528 us; the launch traced here: 521 us
  waiting for transfers between devices  308 us (58%)
  matrix products  123 us (23%)
  other arithmetic  58.6 us (11%)
  between operations  15.7 us (3%)
  local copies, waits for them, and re-layouts  8.2 us (2%)
  blocking collectives  6.46 us (1%)
    psum x1, waiting for transfers between devices, local(): left = lax.psum(partial_value, ('tensor', 'replica')) / replicas  98.4 us
    psum x1, waiting for transfers between devices, local(): lax.psum(lax.psum(v0, shard_axis), mesh_dim)  88.4 us
    psum x1, waiting for transfers between devices, local(): lax.psum(v0, shard_axis)  63.1 us
    all_gather x1, waiting for transfers between devices, local(): lax.all_gather(basis, 'fsdp', axis=1, tiled=True)  37.4 us
    another operation x6, other arithmetic, local(): chol = jnp.linalg.cholesky(gram)  34 us
    dot_general x1, matrix products, local(): jnp.dot(ortho, right.T, precision=HIGH, preferred_element_type=jnp.float32)  33.1 us
    dot_general x1, matrix products, local(): jnp.dot(buffer.T, ortho, precision=HIGH, preferred_element_type=jnp.float32)  31.3 us
    dot_general x1, matrix products, local(): jnp.dot(ortho, basis_full.T, precision=HIGH, preferred_element_type=jnp.f...  28.8 us
  transfers between devices with their start and end apart: 5, of which 5 were waited for; matrix products, arithmetic and copies ran while one was open for 0% of the time, Pallas kernels for 0%

profile of v1, /device:TPU:0, one launch (start us, length us, event | category | flops | bytes accessed | tf_op | source)
XLA Modules:
  0.0 521.1 jit_solution(12921905437739532854)
XLA Ops:
  7.2 0.0 all-gather.2.cloned.1.call-start
  7.2 0.7 all-gather.2.cloned.1.call-update
  7.9 0.0 all-reduce.6.cloned.1.call-start
  7.9 37.4 %all-gather.2.cloned.1.call-done = f32[2048,256]{1,0:T(8,128)} async-done(((f32[2048,128]{1,0:T(8,128)}), f32[2048,256]{1,0:T(8,128)}) %all-gather.2.cloned.1.call-update) | async-done | bytes 2097168 | tf_op jit(solution)/shard_map/all_gather | solution.py:18
  45.3 18.8 %fusion.2 = f32[2048,256]{1,0:T(8,128)} fusion(f32[2048,256]{1,0:T(8,128)} %all-gather.2.cloned.1.call-done, f32[1,2048,2048]{2,1,0:T(8,128)} %param.4, bf16[1,2048,2048]{2,1,0:T(8,128)(2,1)} %param.3), kind=kOutput, calls=%fused_computation.5 | convolution fusion | flops 12893290496 | bytes 29360128 | tf_op jit(solution)/shard_map/dot_general | solution.py:16
  64.2 0.0 all-reduce.6.cloned.1.call-update
  64.2 0.0 all-reduce.8.cloned.1.call-start
  64.3 98.4 %all-reduce.6.cloned.1.call-done = f32[2048,256]{1,0:T(8,128)} async-done(((f32[2048,256]{1,0:T(8,128)}), f32[2048,256]{1,0:T(8,128)}) %all-reduce.6.cloned.1.call-update) | async-done | bytes 2097168 | tf_op jit(solution)/shard_map/psum | solution.py:22
  162.6 6.4 %fusion.19 = f32[256,256]{0,1:T(8,128)} fusion(f32[2048,256]{1,0:T(8,128)} %all-reduce.6.cloned.1.call-done), kind=kOutput, calls=%fused_computation.47 | convolution fusion | flops 1611137024 | bytes 2359296 | tf_op jit(solution)/shard_map/dot_general | solution.py:23
  169.0 0.0 all-reduce.8.cloned.1.call-update
  169.1 0.6 all-reduce.10.cloned.1.call-start
  169.6 1.7 broadcast_multiply_fusion
  171.4 20.4 %all-reduce.8.cloned.1.call-done = f32[256,256]{0,1:T(8,128)} async-done(((f32[256,256]{0,1:T(8,128)}), f32[256,256]{0,1:T(8,128)}) %all-reduce.8.cloned.1.call-update) | async-done | bytes 262160 | tf_op jit(solution)/shard_map/psum | solution.py:24
  191.7 1.1 copy.7
  192.8 1.0 fusion.9
  193.8 11.7 %cholesky.50 = f32[128,128]{1,0:T(8,128)S(1)} custom-call(f32[128,128]{1,0:T(8,128)S(1)} %cholesky.118), custom_call_target="Cholesky" | custom-call | tf_op jit(solution)/shard_map/jit(cholesky)/cholesky | solution.py:25
  205.6 9.8 %custom-call.14 = f32[1,128,128]{1,2,0:T(8,128)S(1)} custom-call(f32[1,128,128]{2,1,0:T(8,128)S(1)} %get-tuple-element.24), custom_call_target="InvertDiagBlocksLowerTriangular" | custom-call | tf_op jit(solution)/shard_map/jit(cholesky)/cholesky | solution.py:25
  215.4 0.2 constant_dynamic-update-slice_fusion
  215.6 0.3 convolution_subtract_fusion.1
  215.9 11.7 %cholesky.105 = f32[128,128]{1,0:T(8,128)S(1)} custom-call(f32[128,128]{1,0:T(8,128)S(1)} %convolution_subtract_fusion.1), custom_call_target="Cholesky" | custom-call | tf_op jit(solution)/shard_map/jit(cholesky)/cholesky | solution.py:25
  227.6 0.6 compare_reduce_fusion
  229.6 0.1 triangular_solve.58
  229.7 4.2 while.1
  229.9 0.6 fusion.28
  230.5 1.4 bitcast_dynamic-update-slice_fusion.2
  231.9 0.6 fusion.28
  232.5 1.4 bitcast_dynamic-update-slice_fusion.2
  233.9 19.7 %custom-call.15 = f32[2,128,128]{1,2,0:T(8,128)S(1)} custom-call(f32[2,128,128]{2,1,0:T(8,128)S(1)} %get-tuple-element.10), custom_call_target="InvertDiagBlocksLowerTriangular" | custom-call | tf_op jit(solution)/shard_map/triangular_solve | solution.py:26
  253.5 1.1 fusion.6
  254.6 1.8 convolution_subtract_fusion
  256.5 1.1 fusion.10
  257.6 0.0 copy-start.1
  257.6 1.0 copy-done.1
  258.5 31.3 %fusion = f32[2048,256]{1,0:T(8,128)} fusion(f32[1,2048,2048]{2,1,0:T(8,128)} %param.4, bf16[1,2048,2048]{2,1,0:T(8,128)(2,1)} %param.3, f32[2048,128]{0,1:T(8,128)S(1)} %fusion.10, f32[2048,128]{0,1:T(8,128)S(1)} %fusion.6), kind=kOutput, calls=%fused_computation.3 | convolution fusion | flops 12893814784 | bytes 29360128 | tf_op jit(solution)/shard_map/dot_general | solution.py:27
  289.8 0.0 all-reduce.10.cloned.1.call-update
  289.8 0.0 all-reduce.12.cloned.1.call-start
  289.9 63.1 %all-reduce.10.cloned.1.call-done = f32[2048,256]{1,0:T(8,128)} async-done(((f32[2048,256]{1,0:T(8,128)}), f32[2048,256]{1,0:T(8,128)}) %all-reduce.10.cloned.1.call-update) | async-done | bytes 2097168 | tf_op jit(solution)/shard_map/psum | solution.py:28
  352.9 0.0 all-reduce.12.cloned.1.call-update
  353.0 88.4 %all-reduce.12.cloned.1.call-done = f32[2048,256]{1,0:T(8,128)} async-done(((f32[2048,256]{1,0:T(8,128)}), f32[2048,256]{1,0:T(8,128)}) %all-reduce.12.cloned.1.call-update) | async-done | bytes 2097168 | tf_op jit(solution)/shard_map/psum | solution.py:28
  441.3 0.0 copy-start
  441.3 2.0 multiply_reduce_fusion
  443.4 6.5 %psum.39 = f32[256]{0:T(256)S(1)} all-reduce(f32[256]{0:T(256)S(1)} %multiply_reduce_fusion), channel_id=1, replica_groups=mesh['fsdp'=2,'tensor'=4,'replica'=4] {'tensor'}, use_global_device_ids=true, to_apply=%region_9.10 | all-reduce | flops 256 | bytes 2048 | tf_op jit(solution)/shard_map/psum | solution.py:30
  449.8 0.0 copy-done
  449.9 0.1 multiply_divide_fusion
  450.0 1.1 copy-done.2
  451.1 28.8 %multiply_convert_fusion = bf16[2048,2048]{1,0:T(8,128)(2,1)} fusion(f32[2048,256]{1,0:T(8,128)S(1)} %multiply_divide_fusion, f32[2048,128]{0,1:T(8,128)S(1)} %copy-done.2, f32[2048,128]{0,1:T(8,128)S(1)} %fusion.6), kind=kOutput, calls=%fused_computation.8 | convolution fusion | flops 12893814784 | bytes 12582912 | tf_op jit(solution)/shard_map/dot_general | solution.py:37
  479.9 1.0 constant_dynamic-slice_fusion.1
  480.9 33.1 %fusion.4 = f32[1,2048,2048]{2,1,0:T(8,128)} fusion(f32[1,2048,2048]{2,1,0:T(8,128)} %param.4, bf16[1,2048,2048]{2,1,0:T(8,128)(2,1)} %param.3, f32[2048,256]{1,0:T(8,128)S(1)} %copy-done, f32[2048,128]{0,1:T(8,128)S(1)} %copy-done.2, f32[2048,128]{0,1:T(8,128)S(1)} %fusion.6), kind=kOutput, calls=%fused_computation.7 | convolution fusion | flops 12902727680 | bytes 46137344 | tf_op jit(solution)/shard_map/dot_general | solution.py:33
  (11 shorter events, 0.2 us)
Async XLA Ops:
  7.2 38.2 %all-gather.2.cloned.1.call-start = ((), (), s32[]{:S(2)}) async-start(), calls=%async_computation | async-start | bytes 3145728 | tf_op jit(solution)/shard_map/all_gather | solution.py:18
  7.9 154.7 %all-reduce.6.cloned.1.call-start = ((), (), s32[]{:S(2)}) async-start(), calls=%async_computation.1 | async-start | bytes 4194304 | tf_op jit(solution)/shard_map/psum | solution.py:22
  64.2 127.5 %all-reduce.8.cloned.1.call-start = ((), (), s32[]{:S(2)}) async-start(), calls=%async_computation.2 | async-start | bytes 524288 | tf_op jit(solution)/shard_map/psum | solution.py:24
  169.1 183.9 %all-reduce.10.cloned.1.call-start = ((), (), s32[]{:S(2)}) async-start(), calls=%async_computation.3 | async-start | bytes 4194304 | tf_op jit(solution)/shard_map/psum | solution.py:28
  257.6 1.0 copy-start.1
  289.8 151.5 %all-reduce.12.cloned.1.call-start = ((), (), s32[]{:S(2)}) async-start(), calls=%async_computation.4 | async-start | bytes 4194304 | tf_op jit(solution)/shard_map/psum | solution.py:28
  441.3 8.5 %copy-start = (f32[2048,256]{1,0:T(8,128)S(1)}, f32[2048,256]{1,0:T(8,128)}, u32[]{:S(2)}) copy-start(f32[2048,256]{1,0:T(8,128)} %all-reduce.12.cloned.1.call-done) | copy-start | bytes 6291460
  449.9 1.2 copy-start.2
Sparse Core Ops, SparseCore 0:
  9.5 35.7 all-gather.1
  64.3 98.2 all-reduce.5
  169.2 22.4 all-reduce.7
  289.9 62.9 all-reduce.9
  355.2 86.1 all-reduce.11
